TPU v7x, 256 devices: a whole 4x4x8 slice. The times are simulated.
256 devices in a mesh: row: 8 (over x, core), col: 32 (over y, z).
Axes of the slice: x: 4, y: 4, z: 8, core: 2. Of those that a mesh axis runs over, the one named last changes fastest.
Arguments:
- hidden: bfloat16 [4096, 8192], P('row', 'col'), may hold values from -600 to 600
- norm_gain: float32 [8192], replicated, may hold values from 0.5 to 2
- wq: bfloat16 [8192, 8192], P('row', 'col'), may hold values from -1 to 1
- wk: bfloat16 [8192, 1024], P('row', 'col'), may hold values from -1 to 1
- wv: bfloat16 [8192, 1024], P('row', 'col'), may hold values from -0.0625 to 0.0625
- wo: bfloat16 [8192, 8192], P('row', 'col'), may hold values from -0.25 to 0.25
Outputs:
- attn_out: bfloat16 [4096, 8192], P('row', 'col')
All inputs are finite; a program needn't handle non-finite values.
Results may differ from a plain program's by a relative error of at most 0.011.
Values may be sent and summed in bfloat16 or wider, within the bound.
A program may use at most 64 MiB of HBM per device.

v0:
```python
import jax
import jax.numpy as jnp
from jax import lax
from jax.sharding import PartitionSpec as P

HD = 128


def partner(array, axis, distance):
    return lax.ppermute(array, axis, [(i, i ^ 1 << distance) for i in range(lax.axis_size(axis))])


def rotary(field, positions):
    half = field.shape[-1] // 2
    steps = jnp.arange(half).astype(jnp.float32)
    freqs = 10000.0 ** (-steps / half)
    angles = positions.astype(jnp.float32)[:, None] * freqs[None, :]
    cosine = jnp.cos(angles)[:, None, :]
    sine = jnp.sin(angles)[:, None, :]
    first = field[..., :half]
    second = field[..., half:]
    return jnp.concatenate(
        [first * cosine - second * sine, second * cosine + first * sine], axis=-1
    )


def order_pair(mine, other, col_index, bit, axis_dim):
    upper = col_index // 2**bit % 2 == 1
    lower_part = jnp.where(upper, other, mine)
    upper_part = jnp.where(upper, mine, other)
    return jnp.concatenate([lower_part, upper_part], axis=axis_dim)


def per_device(hidden, norm_gain, wq, wk, wv, wo):
    tok_rows = hidden.shape[0]
    panel = lax.all_gather(hidden, "col", axis=1, tiled=True)
    values_in = panel.astype(jnp.float32)
    meansq = jnp.mean(values_in * values_in, axis=1, keepdims=True)
    normed = (values_in * lax.rsqrt(meansq + 1e-05) * norm_gain).astype(jnp.bfloat16)
    kv_cols = wk.shape[1]
    group = max(1, HD // kv_cols)
    bits = group.bit_length() - 1
    col_index = lax.axis_index("col")
    stacked = jnp.stack((wk, wv), axis=1)
    for bit in range(bits):
        other = partner(stacked, "col", bit)
        stacked = order_pair(stacked, other, col_index, bit, 2)
    columns = normed
    query_part = jnp.dot(
        columns, lax.all_gather(wq, "row", axis=0, tiled=True), preferred_element_type=jnp.float32
    )
    pair_part = jnp.einsum(
        "ho,omr->hmr",
        columns,
        lax.all_gather(stacked, "row", axis=0, tiled=True),
        preferred_element_type=jnp.float32,
    )
    heads_here = wq.shape[1] // HD
    kv_here = pair_part.shape[2] // HD
    per_kv = heads_here // kv_here
    positions = lax.axis_index("row") * tok_rows + jnp.arange(tok_rows)
    queries = rotary(query_part.reshape(tok_rows, heads_here, HD), positions).astype(jnp.bfloat16)
    queries = queries.reshape(tok_rows, kv_here, per_kv, HD)
    keys = rotary(pair_part[:, 0].reshape(tok_rows, kv_here, HD), positions).astype(jnp.bfloat16)
    values = pair_part[:, 1].reshape(tok_rows, kv_here, HD).astype(jnp.bfloat16)
    scale = HD ** (-0.5)
    best = jnp.full((kv_here, per_kv, tok_rows), -1e30, jnp.float32)
    key_piece = lax.all_gather(keys, "row", axis=0, tiled=True)
    value_piece = lax.all_gather(values, "row", axis=0, tiled=True)
    count = key_piece.shape[0]
    scores = (
        jnp.einsum("tagd,nad->agtn", queries, key_piece, preferred_element_type=jnp.float32) * scale
    )
    key_pos = jnp.arange(count)
    visible = positions[:, None] >= key_pos[None, :]
    scores = jnp.where(visible, scores, -jnp.inf)
    fresh = jnp.maximum(best, jnp.max(scores, axis=3))
    probs = jnp.exp(scores - fresh[..., None])
    total = jnp.sum(probs, axis=3)
    update = jnp.einsum(
        "agtn,nad->agtd",
        probs.astype(jnp.bfloat16),
        value_piece,
        preferred_element_type=jnp.float32,
    )
    numer = update
    best, total, numer = (fresh, total, numer)
    heads = (
        (numer / total[..., None])
        .transpose(2, 0, 1, 3)
        .reshape(tok_rows, heads_here * HD)
        .astype(jnp.bfloat16)
    )
    head_panel = lax.all_gather(heads, "col", axis=1, tiled=True)
    columns = head_panel
    result = jnp.dot(
        columns, lax.all_gather(wo, "row", axis=0, tiled=True), preferred_element_type=jnp.float32
    )
    return result.astype(jnp.bfloat16)


def solution(mesh):
    in_specs = (
        P("row", "col"),
        P(),
        P("row", "col"),
        P("row", "col"),
        P("row", "col"),
        P("row", "col"),
    )
    out_specs = P("row", "col")
    return jax.shard_map(
        per_device, mesh=mesh, in_specs=in_specs, out_specs=out_specs, check_vma=False
    )
```

profile of v0, /device:TPU:1, one launch (start us, length us, event | category | flops | bytes accessed | tf_op | source)
XLA Modules:
  0.0 396.9 jit_solution(9538606364416327431)
XLA Ops:
  6.5 0.0 copy-start.1
  6.5 0.0 all-gather.8.cloned.1.call-start
  6.5 0.7 all-gather.8.cloned.1.call-update
  7.3 0.0 all-gather.10.cloned.1.call-start
  7.3 0.9 pad_maximum_fusion.2
  8.2 2.6 collective-permute-start
  10.7 2.4 collective-permute-done
  13.1 0.9 broadcast_select_fusion.3
  14.0 3.8 collective-permute-start.1
  17.9 11.3 %collective-permute-done.1 = bf16[1024,2,64]{0,2,1:T(8,128)(2,1)S(1)} collective-permute-done((bf16[1024,2,64]{0,2,1:T(8,128)(2,1)S(1)}, bf16[1024,2,64]{0,2,1:T(8,128)(2,1)S(1)}, u32[]{:S(2)}, u32[]{:S(2)}) %collective-permute-start.1) | collective-permute-done | bytes 262176 | tf_op jit(solution)/shard_map/ppermute | solution.py:10
  29.2 0.1 broadcast_select_fusion.1
  29.3 0.8 pad_maximum_fusion
  30.1 0.0 all-gather.10.cloned.1.call-update
  30.2 0.0 all-gather.14.cloned.1.call-start
  30.2 0.7 all-gather.14.cloned.1.call-update
  30.9 0.0 all-gather.12.cloned.1.call-start
  31.0 86.2 %all-gather.8.cloned.1.call-done = bf16[512,8192]{1,0:T(8,128)(2,1)} async-done(((bf16[512,256]{1,0:T(8,128)(2,1)}), bf16[512,8192]{1,0:T(8,128)(2,1)}) %all-gather.8.cloned.1.call-update) | async-done | bytes 8388624 | tf_op jit(solution)/shard_map/all_gather | solution.py:36
  117.1 5.1 %fusion = f32[512]{0:T(512)S(1)} fusion(bf16[512,8192]{1,0:T(8,128)(2,1)} %all-gather.8.cloned.1.call-done), kind=kLoop, calls=%fused_computation.2 | loop fusion | flops 12582400 | bytes 8390656 | tf_op jit(solution)/shard_map/reduce_sum | solution.py:38
  122.3 31.8 %all-gather.10.cloned.1.call-done = bf16[8192,2,128]{0,2,1:T(8,128)(2,1)} async-done(((bf16[1024,2,128]{0,2,1:T(8,128)(2,1)}), bf16[8192,2,128]{0,2,1:T(8,128)(2,1)}) %all-gather.10.cloned.1.call-update) | async-done | bytes 4194320 | tf_op jit(solution)/shard_map/all_gather | solution.py:55
  154.1 0.0 copy-done.1
  154.1 7.0 %fusion.12 = f32[512,256]{0,1:S(1)} fusion(bf16[8192,256]{0,1:T(8,128)(2,1)} %bitcast.61, bf16[512,8192]{1,0:T(8,128)(2,1)} %all-gather.8.cloned.1.call-done, f32[8192]{0:T(1024)S(1)} %copy-done.1, f32[512]{0:T(512)S(1)} %add_rsqrt_fusion), kind=kOutput, calls=%fused_computation.15 | convolution fusion | flops 2164260864 | bytes 13142016
  161.1 0.6 fusion.35
  161.7 0.7 pad_maximum_fusion.3
  162.4 0.0 all-gather.12.cloned.1.call-update
  162.4 0.0 all-gather.16.cloned.1.call-start
  162.4 0.7 slice.34
  163.1 0.0 all-gather.16.cloned.1.call-update
  163.1 0.0 all-gather.20.cloned.1.call-start
  163.2 0.5 all-gather.20.cloned.1.call-update
  163.7 0.2 all-gather.18.cloned.1.call-start
  163.9 1.8 multiply_cosine_fusion
  165.7 1.7 iota_compare_fusion
  167.5 23.2 %all-gather.14.cloned.1.call-done = bf16[8192,256]{1,0:T(8,128)(2,1)} async-done(((bf16[1024,256]{1,0:T(8,128)(2,1)}), bf16[8192,256]{1,0:T(8,128)(2,1)}) %all-gather.14.cloned.1.call-update) | async-done | bytes 4194320 | tf_op jit(solution)/shard_map/all_gather | solution.py:50
  190.6 7.6 %fusion.10 = f32[512,256]{0,1:T(8,128)S(1)} fusion(bf16[8192,256]{1,0:T(8,128)(2,1)} %all-gather.14.cloned.1.call-done, bf16[512,8192]{1,0:T(8,128)(2,1)} %all-gather.8.cloned.1.call-done, f32[8192]{0:T(1024)S(1)} %copy-done.1, f32[512]{0:T(512)S(1)} %add_rsqrt_fusion), kind=kOutput, calls=%fused_computation.14 | convolution fusion | flops 2164260864 | bytes 13142016 | tf_op jit(solution)/shard_map/dot_general | solution.py:49
  198.3 0.2 copy.14
  198.5 0.2 copy.15
  198.7 1.9 subtract_convert_fusion
  200.5 17.7 %all-gather.12.cloned.1.call-done = bf16[4096,1,128]{0,2,1:T(8,128)(2,1)} async-done(((bf16[512,1,128]{0,2,1:T(8,128)(2,1)}), bf16[4096,1,128]{0,2,1:T(8,128)(2,1)}) %all-gather.12.cloned.1.call-update) | async-done | bytes 1048592 | tf_op jit(solution)/shard_map/all_gather | solution.py:68
  218.2 5.1 %fusion.5 = (f32[2,512]{1,0:T(2,128)S(1)}, f32[4096,512,2]{1,0,2:T(8,128)S(1)}) fusion(pred[512,4096]{0,1:T(8,128)(4,1)S(1)} %iota_compare_fusion, bf16[512,2,64]{2,0,1:T(8,128)(2,1)} %get-tuple-element.6, bf16[512,2,64]{2,0,1:T(8,128)(2,1)S(1)} %get-tuple-element.5, bf16[4096,1,128]{0,2,1:T(8,128)(2,1)} %all-gather.12.cloned.1.call-done), kind=kOutput, calls=%fused_computation.9 | convolution fusion | flops 1086848000 | bytes 20189184 | tf_op jit(solution)/shard_map/tagd,nad->agtn/dot_general | solution.py:72
  223.3 0.0 copy-start
  223.3 5.7 %copy-done = f32[4096,512,2]{1,0,2:T(8,128)} copy-done((f32[4096,512,2]{1,0,2:T(8,128)}, f32[4096,512,2]{1,0,2:T(8,128)S(1)}, u32[]{:S(2)}) %copy-start) | copy-done | bytes 16777240
  229.0 4.2 %fusion.3 = f32[2,512]{1,0:T(2,128)S(1)} fusion(f32[4096,512,2]{1,0,2:T(8,128)S(1)} %get-tuple-element.18, f32[2,512]{1,0:T(2,128)S(1)} %broadcast_maximum_fusion, pred[512,4096]{0,1:T(8,128)(4,1)S(1)} %iota_compare_fusion), kind=kLoop, calls=%fused_computation.7 | loop fusion | flops 16776192 | bytes 18882560 | tf_op jit(solution)/shard_map/reduce_sum | solution.py:79
  233.2 12.6 %all-gather.16.cloned.1.call-done = bf16[4096,1,128]{0,2,1:T(8,128)(2,1)} async-done(((bf16[512,1,128]{0,2,1:T(8,128)(2,1)}), bf16[4096,1,128]{0,2,1:T(8,128)(2,1)}) %all-gather.16.cloned.1.call-update) | async-done | bytes 1048592 | tf_op jit(solution)/shard_map/all_gather | solution.py:69
  245.8 11.7 %fusion.22 = bf16[2,512,128]{1,2,0:T(8,128)(2,1)} fusion(f32[4096,512,2]{1,0,2:T(8,128)} %copy-done, f32[2,512]{1,0:T(2,128)S(1)} %broadcast_maximum_fusion, pred[512,4096]{0,1:T(8,128)(4,1)S(1)} %iota_compare_fusion, bf16[4096,1,128]{0,2,1:T(8,128)(2,1)} %all-gather.16.cloned.1.call-done, f32[2,512]{1,0:T(2,128)S(1)} %fusion.3), kind=kOutput, calls=%fused_computation.21 | convolution fusion | flops 1090781184 | bytes 20193280 | tf_op jit(solution)/shard_map/agtn,nad->agtd/dot_general | solution.py:80
  257.4 0.0 all-gather.18.cloned.1.call-update
  257.4 24.6 %all-gather.20.cloned.1.call-done = bf16[8192,256]{1,0:T(8,128)(2,1)} async-done(((bf16[1024,256]{1,0:T(8,128)(2,1)}), bf16[8192,256]{1,0:T(8,128)(2,1)}) %all-gather.20.cloned.1.call-update) | async-done | bytes 4194320 | tf_op jit(solution)/shard_map/all_gather | solution.py:97
  282.0 100.3 %all-gather.18.cloned.1.call-done = bf16[512,8192]{0,1:T(8,128)(2,1)} async-done(((bf16[512,256]{0,1:T(8,128)(2,1)}), bf16[512,8192]{0,1:T(8,128)(2,1)}) %all-gather.18.cloned.1.call-update) | async-done | bytes 8388624 | tf_op jit(solution)/shard_map/all_gather | solution.py:94
  382.4 7.7 %convolution_convert_fusion = bf16[512,256]{1,0:T(8,128)(2,1)} fusion(bf16[512,8192]{0,1:T(8,128)(2,1)} %all-gather.18.cloned.1.call-done, bf16[8192,256]{1,0:T(8,128)(2,1)} %all-gather.20.cloned.1.call-done), kind=kOutput, calls=%fused_computation.16 | convolution fusion | flops 2147614720 | bytes 12845056 | tf_op jit(solution)/shard_map/dot_general | solution.py:96
  (7 shorter events, 0.1 us)
Async XLA Ops:
  6.5 147.6 %copy-start.1 = (f32[8192]{0:T(1024)S(1)}, f32[8192]{0:T(1024)}, u32[]{:S(2)}) copy-start(f32[8192]{0:T(1024)} %param.7) | copy-start | bytes 98308
  6.5 110.6 %all-gather.8.cloned.1.call-start = ((), (), s32[]{:S(2)}) async-start(), calls=%async_computation | async-start | bytes 8650752 | tf_op jit(solution)/shard_map/all_gather | solution.py:36
  7.3 146.8 %all-gather.10.cloned.1.call-start = ((), (), s32[]{:S(2)}) async-start(), calls=%async_computation.1 | async-start | bytes 4718592 | tf_op jit(solution)/shard_map/all_gather | solution.py:55
  8.2 4.9 %collective-permute-start = (bf16[1024,2,32]{0,2,1:T(8,128)(2,1)S(1)}, bf16[1024,2,32]{0,2,1:T(8,128)(2,1)S(1)}, u32[]{:S(2)}, u32[]{:S(2)}) collective-permute-start(bf16[1024,2,32]{0,2,1:T(8,128)(2,1)S(1)} %pad_maximum_fusion.2), channel_id=1, source_target_pairs={{0,1},{1,0},{2,3},{3,2},{4,5},{5,4},{6,7},{7,6},{8,9},{9,8},{10,11... | collective-permute-start | bytes 393224 | tf_op jit(solution)/shard_map/ppermute | solution.py:10
  14.0 15.2 %collective-permute-start.1 = (bf16[1024,2,64]{0,2,1:T(8,128)(2,1)S(1)}, bf16[1024,2,64]{0,2,1:T(8,128)(2,1)S(1)}, u32[]{:S(2)}, u32[]{:S(2)}) collective-permute-start(bf16[1024,2,64]{0,2,1:T(8,128)(2,1)S(1)} %pad_maximum_fusion.1), channel_id=1, source_target_pairs={{0,2},{1,3},{2,0},{3,1},{4,6},{5,7},{6,4},{7,5},{8,10},{9,11},{10,... | collective-permute-start | bytes 786440 | tf_op jit(solution)/shard_map/ppermute | solution.py:10
  30.2 160.5 %all-gather.14.cloned.1.call-start = ((), (), s32[]{:S(2)}) async-start(), calls=%async_computation.3 | async-start | bytes 4718592 | tf_op jit(solution)/shard_map/all_gather | solution.py:50
  30.9 187.3 %all-gather.12.cloned.1.call-start = ((), (), s32[]{:S(2)}) async-start(), calls=%async_computation.2 | async-start | bytes 1179648 | tf_op jit(solution)/shard_map/all_gather | solution.py:68
  162.4 83.4 %all-gather.16.cloned.1.call-start = ((), (), s32[]{:S(2)}) async-start(), calls=%async_computation.4 | async-start | bytes 1179648 | tf_op jit(solution)/shard_map/all_gather | solution.py:69
  163.1 118.9 %all-gather.20.cloned.1.call-start = ((), (), s32[]{:S(2)}) async-start(), calls=%async_computation.6 | async-start | bytes 4718592 | tf_op jit(solution)/shard_map/all_gather | solution.py:97
  163.7 218.7 %all-gather.18.cloned.1.call-start = ((), (), s32[]{:S(2)}) async-start(), calls=%async_computation.5 | async-start | bytes 8650752 | tf_op jit(solution)/shard_map/all_gather | solution.py:94
  223.3 5.7 %copy-start = (f32[4096,512,2]{1,0,2:T(8,128)}, f32[4096,512,2]{1,0,2:T(8,128)S(1)}, u32[]{:S(2)}) copy-start(f32[4096,512,2]{1,0,2:T(8,128)S(1)} %get-tuple-element.18) | copy-start | bytes 50331652
Sparse Core Ops, SparseCore 0:
  9.8 107.2 all-gather.7
  119.0 35.0 all-gather.9
  156.0 34.6 all-gather.13
  192.3 25.8 all-gather.11
  219.9 25.7 all-gather.15
  247.5 34.5 all-gather.19
  284.6 97.6 all-gather.17
where the time goes:
time: 397 us
  waiting for transfers between devices  312 us (79%)
  matrix products  39 us (10%)
  other arithmetic  18.7 us (5%)
  between operations  13.6 us (3%)
  local copies, waits for them, and re-layouts  6.8 us (2%)
  starting transfers between devices  6.8 us (2%)
    all_gather x1, waiting for transfers between devices, per_device(): head_panel = lax.all_gather(heads, 'col', axis=1, tiled=True)  100 us
    all_gather x1, waiting for transfers between devices, per_device(): panel = lax.all_gather(hidden, 'col', axis=1, tiled=True)  86.2 us
    all_gather x1, waiting for transfers between devices, per_device(): lax.all_gather(stacked, 'row', axis=0, tiled=True)  31.8 us
    all_gather x1, waiting for transfers between devices, per_device(): lax.all_gather(wo, 'row', axis=0, tiled=True)  24.6 us
    all_gather x1, waiting for transfers between devices, per_device(): lax.all_gather(wq, 'row', axis=0, tiled=True)  23.2 us
    all_gather x1, waiting for transfers between devices, per_device(): key_piece = lax.all_gather(keys, 'row', axis=0, tiled=True)  17.7 us
    ppermute x2, waiting for transfers between devices, partner(): lax.ppermute(array, axis, [(i, i ^ 1 << distance) for i in range(lax.axis...  13.7 us
    all_gather x1, waiting for transfers between devices, per_device(): value_piece = lax.all_gather(values, 'row', axis=0, tiled=True)  12.6 us
  transfers between devices with their start and end apart: 9, of which 9 were waited for; matrix products, arithmetic and copies ran while one was open for 13% of the time, Pallas kernels for 0%

commit v1 on v0

--- a/solution.py
+++ b/solution.py
@@ -1,9 +1,32 @@
+import functools
 import jax
 import jax.numpy as jnp
 from jax import lax
 from jax.sharding import PartitionSpec as P
 
 HD = 128
+
+
+def watch_the_sectors(local_x, dimension_no):
+    world_n = jax.lax.psum(1, "row")
+    found = []
+    for s in [*range(world_n)]:
+        found.append((s, (s + 1) % world_n))
+
+    def windows_recover(field_out):
+        if len(field_out) == world_n:
+            return field_out
+        block_next = windows_recover([jax.lax.ppermute(field_out[0], "row", found), *field_out])
+        return block_next
+
+    x_now = jnp.concatenate(windows_recover([local_x]), dimension_no)
+    piece_out = jnp.roll(
+        x_now, (jax.lax.axis_index("row") + 1) * local_x.shape[dimension_no], dimension_no
+    )
+    return piece_out
+
+
+keep_up_outputs = functools.partial(watch_the_sectors, dimension_no=0)
 
 
 def partner(array, axis, distance):
@@ -66,7 +89,7 @@
     scale = HD ** (-0.5)
     best = jnp.full((kv_here, per_kv, tok_rows), -1e30, jnp.float32)
     key_piece = lax.all_gather(keys, "row", axis=0, tiled=True)
-    value_piece = lax.all_gather(values, "row", axis=0, tiled=True)
+    value_piece = keep_up_outputs(values)
     count = key_piece.shape[0]
     scores = (
         jnp.einsum("tagd,nad->agtn", queries, key_piece, preferred_element_type=jnp.float32) * scale

time: 397 us -> 374 us (0.942)
  waiting for transfers between devices: 312 us -> 279 us
  starting transfers between devices: 6.8 us -> 17.3 us
  matrix products: 39 us -> 34.4 us
  local copies, waits for them, and re-layouts: 6.8 us -> 11.4 us
    all_gather x1, waiting for transfers between devices: 17.7 us -> 1.25 us  [per_device(): key_piece = lax.all_gather(keys, 'row', axis=0, tiled=True)]
    ppermute x0 -> x7, waiting for transfers between devices: none -> 15.5 us  [windows_recover(): jax.lax.ppermute(field_out[0], 'row', found)]
    all_gather x1, waiting for transfers between devices: 23.2 us -> 8.27 us  [per_device(): lax.all_gather(wq, 'row', axis=0, tiled=True)]
    all_gather x1 -> x0, waiting for transfers between devices: 12.6 us -> none  [per_device(): value_piece = lax.all_gather(values, 'row', axis=0, tiled=True)]
    ppermute x0 -> x7, starting transfers between devices: none -> 10.7 us  [windows_recover(): jax.lax.ppermute(field_out[0], 'row', found)]
    dot_general x1, matrix products: 11.7 us -> 6.44 us  [per_device(): jnp.einsum('agtn,nad->agtd', probs.astype(jnp.bfloat16), value_piece, pre...]
    unnamed x6 -> x21, local copies, waits for them, and re-layouts: 6.1 us -> 10.7 us
    all_gather x1, waiting for transfers between devices: 24.6 us -> 20.4 us  [per_device(): lax.all_gather(wo, 'row', axis=0, tiled=True)]
  transfers between devices with their start and end apart: 9 -> 15, of which waited for: 9 -> 14; matrix products, arithmetic and copies ran while one was open for 13% -> 15% of each run, Pallas kernels for 0% -> 0%
where the time goes in v1:
time: 374 us; the launch traced here: 373 us
  waiting for transfers between devices  279 us (75%)
  matrix products  34.4 us (9%)
  other arithmetic  17.9 us (5%)
  starting transfers between devices  17.3 us (5%)
  between operations  13.7 us (4%)
  local copies, waits for them, and re-layouts  11.4 us (3%)
    all_gather x1, waiting for transfers between devices, per_device(): head_panel = lax.all_gather(heads, 'col', axis=1, tiled=True)  100 us
    all_gather x1, waiting for transfers between devices, per_device(): panel = lax.all_gather(hidden, 'col', axis=1, tiled=True)  86.1 us
    all_gather x1, waiting for transfers between devices, per_device(): lax.all_gather(stacked, 'row', axis=0, tiled=True)  31.8 us
    all_gather x1, waiting for transfers between devices, per_device(): lax.all_gather(wo, 'row', axis=0, tiled=True)  20.4 us
    ppermute x7, waiting for transfers between devices, windows_recover(): jax.lax.ppermute(field_out[0], 'row', found)  15.5 us
    ppermute x2, waiting for transfers between devices, partner(): lax.ppermute(array, axis, [(i, i ^ 1 << distance) for i in range(lax.axis...  13.7 us
    ppermute x7, starting transfers between devices, windows_recover(): jax.lax.ppermute(field_out[0], 'row', found)  10.7 us
    unnamed x21, local copies, waits for them, and re-layouts  10.7 us
  transfers between devices with their start and end apart: 15, of which 14 were waited for; matrix products, arithmetic and copies ran while one was open for 15% of the time, Pallas kernels for 0%

profile of v1, /device:TPU:1, one launch (start us, length us, event | category | flops | bytes accessed | tf_op | source)
XLA Modules:
  0.0 373.4 jit_solution(7736142410809775746)
XLA Ops:
  6.5 0.7 all-gather.7.cloned.1.call-update
  7.3 0.0 all-gather.9.cloned.1.call-start
  7.3 0.9 pad_maximum_fusion.2
  8.2 2.6 collective-permute-start
  10.7 2.4 collective-permute-done
  13.1 0.9 broadcast_select_fusion.3
  14.0 3.8 %collective-permute-start.1 = (bf16[1024,2,64]{0,2,1:T(8,128)(2,1)S(1)}, bf16[1024,2,64]{0,2,1:T(8,128)(2,1)S(1)}, u32[]{:S(2)}, u32[]{:S(2)}) collective-permute-start(bf16[1024,2,64]{0,2,1:T(8,128)(2,1)S(1)} %pad_maximum_fusion.1), channel_id=1, source_target_pairs={{0,2},{1,3},{2,0},{3,1},{4,6},{5,7},{6,4},{7,5},{8,10},{9,11},{10,... | collective-permute-start | bytes 786440 | tf_op jit(solution)/shard_map/ppermute | solution.py:33
  17.9 11.3 %collective-permute-done.1 = bf16[1024,2,64]{0,2,1:T(8,128)(2,1)S(1)} collective-permute-done((bf16[1024,2,64]{0,2,1:T(8,128)(2,1)S(1)}, bf16[1024,2,64]{0,2,1:T(8,128)(2,1)S(1)}, u32[]{:S(2)}, u32[]{:S(2)}) %collective-permute-start.1) | collective-permute-done | bytes 262176 | tf_op jit(solution)/shard_map/ppermute | solution.py:33
  29.2 0.1 broadcast_select_fusion.1
  29.3 0.8 pad_maximum_fusion
  30.2 0.0 all-gather.9.cloned.1.call-update
  30.2 0.0 all-gather.13.cloned.1.call-start
  30.2 0.7 all-gather.13.cloned.1.call-update
  30.9 0.0 all-gather.11.cloned.1.call-start
  31.0 86.1 %all-gather.7.cloned.1.call-done = bf16[512,8192]{1,0:T(8,128)(2,1)} async-done(((bf16[512,256]{1,0:T(8,128)(2,1)}), bf16[512,8192]{1,0:T(8,128)(2,1)}) %all-gather.7.cloned.1.call-update) | async-done | bytes 8388624 | tf_op jit(solution)/shard_map/all_gather | solution.py:59
  117.1 5.1 %fusion = f32[512]{0:T(512)S(1)} fusion(bf16[512,8192]{1,0:T(8,128)(2,1)} %all-gather.7.cloned.1.call-done), kind=kLoop, calls=%fused_computation.2 | loop fusion | flops 12582400 | bytes 8390656 | tf_op jit(solution)/shard_map/reduce_sum | solution.py:61
  122.3 31.8 %all-gather.9.cloned.1.call-done = bf16[8192,2,128]{0,2,1:T(8,128)(2,1)} async-done(((bf16[1024,2,128]{0,2,1:T(8,128)(2,1)}), bf16[8192,2,128]{0,2,1:T(8,128)(2,1)}) %all-gather.9.cloned.1.call-update) | async-done | bytes 4194320 | tf_op jit(solution)/shard_map/all_gather | solution.py:78
  154.1 7.0 %fusion.12 = f32[512,256]{0,1:S(1)} fusion(bf16[8192,256]{0,1:T(8,128)(2,1)} %bitcast.63, bf16[512,8192]{1,0:T(8,128)(2,1)} %all-gather.7.cloned.1.call-done, f32[8192]{0:T(1024)S(1)} %copy-done.1, f32[512]{0:T(512)S(1)} %add_rsqrt_fusion), kind=kOutput, calls=%fused_computation.15 | convolution fusion | flops 2164260864 | bytes 13142016
  161.1 0.6 fusion.36
  161.7 0.7 pad_maximum_fusion.3
  162.4 0.0 all-gather.17.cloned.1.call-start
  162.4 0.3 collective-permute-start.2
  162.8 1.9 collective-permute-done.2
  164.7 2.4 collective-permute-start.3
  167.2 0.0 all-gather.15.cloned.1.call-start
  167.3 2.3 collective-permute-done.3
  169.6 2.6 collective-permute-start.4
  172.2 3.0 iota_compare_fusion
  175.3 2.1 collective-permute-done.4
  177.4 2.0 collective-permute-start.5
  179.4 1.0 multiply_cosine_fusion
  180.4 5.4 %collective-permute-done.5 = bf16[512,1,128]{0,2,1:T(8,128)(2,1)S(1)} collective-permute-done((bf16[512,1,128]{0,2,1:T(8,128)(2,1)S(1)}, bf16[512,1,128]{0,2,1:T(8,128)(2,1)S(1)}, u32[]{:S(2)}, u32[]{:S(2)}) %collective-permute-start.5) | collective-permute-done | bytes 131104 | tf_op jit(solution)/shard_map/ppermute | solution.py:19
  185.8 0.8 collective-permute-start.6
  186.6 8.3 %all-gather.13.cloned.1.call-done = bf16[8192,256]{1,0:T(8,128)(2,1)} async-done(((bf16[1024,256]{1,0:T(8,128)(2,1)}), bf16[8192,256]{1,0:T(8,128)(2,1)}) %all-gather.13.cloned.1.call-update) | async-done | bytes 4194320 | tf_op jit(solution)/shard_map/all_gather | solution.py:73
  194.8 7.6 %fusion.10 = f32[512,256]{0,1:T(8,128)S(1)} fusion(bf16[8192,256]{1,0:T(8,128)(2,1)} %all-gather.13.cloned.1.call-done, bf16[512,8192]{1,0:T(8,128)(2,1)} %all-gather.7.cloned.1.call-done, f32[8192]{0:T(1024)S(1)} %copy-done.1, f32[512]{0:T(512)S(1)} %add_rsqrt_fusion), kind=kOutput, calls=%fused_computation.14 | convolution fusion | flops 2164260864 | bytes 13142016 | tf_op jit(solution)/shard_map/dot_general | solution.py:72
  202.5 0.2 copy.14
  202.7 0.2 copy.15
  202.9 1.5 collective-permute-done.7
  204.4 2.4 collective-permute-start.8
  206.8 0.8 subtract_convert_fusion
  207.7 2.2 collective-permute-done.8
  209.9 0.7 constant_dynamic-update-slice_fusion.15
  210.6 0.7 constant_dynamic-update-slice_fusion.14
  211.2 0.7 constant_dynamic-update-slice_fusion.13
  211.9 0.7 constant_dynamic-update-slice_fusion.12
  212.6 0.7 constant_dynamic-update-slice_fusion.11
  213.3 0.7 constant_dynamic-update-slice_fusion.10
  214.0 0.7 constant_dynamic-update-slice_fusion.9
  214.6 0.7 constant_dynamic-update-slice_fusion.8
  215.3 0.7 constant_dynamic-update-slice_fusion.7
  216.0 0.7 constant_dynamic-update-slice_fusion.6
  216.7 0.7 constant_dynamic-update-slice_fusion.5
  217.4 0.7 constant_dynamic-update-slice_fusion.4
  218.1 0.7 constant_dynamic-update-slice_fusion.3
  218.8 0.7 constant_dynamic-update-slice_fusion.2
  219.4 0.7 constant_dynamic-update-slice_fusion.1
  220.1 0.7 constant_dynamic-update-slice_fusion
  220.9 1.3 all-gather.11.cloned.1.call-done
  222.1 5.7 %fusion.5 = (f32[2,512]{1,0:T(2,128)S(1)}, f32[4096,512,2]{1,0,2:T(8,128)S(1)}) fusion(pred[512,4096]{0,1:T(8,128)(4,1)} %iota_compare_fusion, bf16[512,2,64]{2,0,1:T(8,128)(2,1)} %get-tuple-element.6, bf16[512,2,64]{2,0,1:T(8,128)(2,1)S(1)} %get-tuple-element.5, bf16[4096,1,128]{0,2,1:T(8,128)(2,1)} %all-gather.11.cloned.1.call-done), kind=kOutput, calls=%fused_computation.9 | convolution fusion | flops 1086848000 | bytes 20189184 | tf_op jit(solution)/shard_map/tagd,nad->agtn/dot_general | solution.py:95
  227.8 4.0 %fusion.3 = f32[2,512]{1,0:T(2,128)S(1)} fusion(f32[4096,512,2]{1,0,2:T(8,128)S(1)} %get-tuple-element.18, f32[2,512]{1,0:T(2,128)S(1)} %broadcast_maximum_fusion, pred[512,4096]{0,1:T(8,128)(4,1)S(1)} %copy-done), kind=kLoop, calls=%fused_computation.7 | loop fusion | flops 16776192 | bytes 18882560 | tf_op jit(solution)/shard_map/reduce_sum | solution.py:102
  231.8 6.4 %fusion.23 = bf16[2,512,128]{1,2,0:T(8,128)(2,1)} fusion(f32[4096,512,2]{1,0,2:T(8,128)S(1)} %get-tuple-element.18, f32[2,512]{1,0:T(2,128)S(1)} %broadcast_maximum_fusion, pred[512,4096]{0,1:T(8,128)(4,1)} %iota_compare_fusion, bf16[8192,1,128]{0,2,1:T(8,128)(2,1)} %constant_dynamic-update-slice_fusion, s32[]{:T(128)S(6)} %select_n.67, f32[2,512]{1,0:T(2,128)S(1)} %fusion.3), kind=kOutput, calls=%fused_computation.22 | convolution fusion | flops 1090781184 | bytes 20193284 | tf_op jit(solution)/shard_map/agtn,nad->agtd/dot_general | solution.py:103
  238.3 20.4 %all-gather.17.cloned.1.call-done = bf16[8192,256]{1,0:T(8,128)(2,1)} async-done(((bf16[1024,256]{1,0:T(8,128)(2,1)}), bf16[8192,256]{1,0:T(8,128)(2,1)}) %all-gather.17.cloned.1.call-update) | async-done | bytes 4194320 | tf_op jit(solution)/shard_map/all_gather | solution.py:120
  258.7 100.2 %all-gather.15.cloned.1.call-done = bf16[512,8192]{0,1:T(8,128)(2,1)} async-done(((bf16[512,256]{0,1:T(8,128)(2,1)}), bf16[512,8192]{0,1:T(8,128)(2,1)}) %all-gather.15.cloned.1.call-update) | async-done | bytes 8388624 | tf_op jit(solution)/shard_map/all_gather | solution.py:117
  358.9 7.7 %convolution_convert_fusion = bf16[512,256]{1,0:T(8,128)(2,1)} fusion(bf16[512,8192]{0,1:T(8,128)(2,1)} %all-gather.15.cloned.1.call-done, bf16[8192,256]{1,0:T(8,128)(2,1)} %all-gather.17.cloned.1.call-done), kind=kOutput, calls=%fused_computation.16 | convolution fusion | flops 2147614720 | bytes 12845056 | tf_op jit(solution)/shard_map/dot_general | solution.py:119
  (18 shorter events, 0.2 us)
Async XLA Ops:
  6.5 110.6 %all-gather.7.cloned.1.call-start = ((), (), s32[]{:S(2)}) async-start(), calls=%async_computation | async-start | bytes 8650752 | tf_op jit(solution)/shard_map/all_gather | solution.py:59
  7.3 146.8 %all-gather.9.cloned.1.call-start = ((), (), s32[]{:S(2)}) async-start(), calls=%async_computation.1 | async-start | bytes 4718592 | tf_op jit(solution)/shard_map/all_gather | solution.py:78
  8.2 4.9 %collective-permute-start = (bf16[1024,2,32]{0,2,1:T(8,128)(2,1)S(1)}, bf16[1024,2,32]{0,2,1:T(8,128)(2,1)S(1)}, u32[]{:S(2)}, u32[]{:S(2)}) collective-permute-start(bf16[1024,2,32]{0,2,1:T(8,128)(2,1)S(1)} %pad_maximum_fusion.2), channel_id=1, source_target_pairs={{0,1},{1,0},{2,3},{3,2},{4,5},{5,4},{6,7},{7,6},{8,9},{9,8},{10,11... | collective-permute-start | bytes 393224 | tf_op jit(solution)/shard_map/ppermute | solution.py:33
  14.0 15.2 %collective-permute-start.1 = (bf16[1024,2,64]{0,2,1:T(8,128)(2,1)S(1)}, bf16[1024,2,64]{0,2,1:T(8,128)(2,1)S(1)}, u32[]{:S(2)}, u32[]{:S(2)}) collective-permute-start(bf16[1024,2,64]{0,2,1:T(8,128)(2,1)S(1)} %pad_maximum_fusion.1), channel_id=1, source_target_pairs={{0,2},{1,3},{2,0},{3,1},{4,6},{5,7},{6,4},{7,5},{8,10},{9,11},{10,... | collective-permute-start | bytes 786440 | tf_op jit(solution)/shard_map/ppermute | solution.py:33
  30.2 164.7 %all-gather.13.cloned.1.call-start = ((), (), s32[]{:S(2)}) async-start(), calls=%async_computation.3 | async-start | bytes 4718592 | tf_op jit(solution)/shard_map/all_gather | solution.py:73
  30.9 191.2 %all-gather.11.cloned.1.call-start = ((), (), s32[]{:S(2)}) async-start(), calls=%async_computation.2 | async-start | bytes 1179648 | tf_op jit(solution)/shard_map/all_gather | solution.py:91
  31.0 123.1 %copy-start.1 = (f32[8192]{0:T(1024)S(1)}, f32[8192]{0:T(1024)}, u32[]{:S(2)}) copy-start(f32[8192]{0:T(1024)} %param.7) | copy-start | bytes 98308
  162.4 96.4 %all-gather.17.cloned.1.call-start = ((), (), s32[]{:S(2)}) async-start(), calls=%async_computation.5 | async-start | bytes 4718592 | tf_op jit(solution)/shard_map/all_gather | solution.py:120
  162.4 2.3 collective-permute-start.2
  164.7 4.9 %collective-permute-start.3 = (bf16[512,1,128]{0,2,1:T(8,128)(2,1)S(1)}, bf16[512,1,128]{0,2,1:T(8,128)(2,1)S(1)}, u32[]{:S(2)}, u32[]{:S(2)}) collective-permute-start(bf16[512,1,128]{0,2,1:T(8,128)(2,1)S(1)} %collective-permute-done.2), channel_id=1, source_target_pairs={{0,32},{32,64},{64,96},{96,128},{128,160},{160,192},{192,224},{224... | collective-permute-start | bytes 393224 | tf_op jit(solution)/shard_map/ppermute | solution.py:19
  167.2 191.7 %all-gather.15.cloned.1.call-start = ((), (), s32[]{:S(2)}) async-start(), calls=%async_computation.4 | async-start | bytes 8650752 | tf_op jit(solution)/shard_map/all_gather | solution.py:117
  169.6 7.8 %collective-permute-start.4 = (bf16[512,1,128]{0,2,1:T(8,128)(2,1)S(1)}, bf16[512,1,128]{0,2,1:T(8,128)(2,1)S(1)}, u32[]{:S(2)}, u32[]{:S(2)}) collective-permute-start(bf16[512,1,128]{0,2,1:T(8,128)(2,1)S(1)} %collective-permute-done.3), channel_id=1, source_target_pairs={{0,32},{32,64},{64,96},{96,128},{128,160},{160,192},{192,224},{224... | collective-permute-start | bytes 393224 | tf_op jit(solution)/shard_map/ppermute | solution.py:19
  177.4 8.4 %collective-permute-start.5 = (bf16[512,1,128]{0,2,1:T(8,128)(2,1)S(1)}, bf16[512,1,128]{0,2,1:T(8,128)(2,1)S(1)}, u32[]{:S(2)}, u32[]{:S(2)}) collective-permute-start(bf16[512,1,128]{0,2,1:T(8,128)(2,1)S(1)} %collective-permute-done.4), channel_id=1, source_target_pairs={{0,32},{32,64},{64,96},{96,128},{128,160},{160,192},{192,224},{224... | collective-permute-start | bytes 393224 | tf_op jit(solution)/shard_map/ppermute | solution.py:19
  185.8 16.6 %collective-permute-start.6 = (bf16[512,1,128]{0,2,1:T(8,128)(2,1)S(1)}, bf16[512,1,128]{0,2,1:T(8,128)(2,1)S(1)}, u32[]{:S(2)}, u32[]{:S(2)}) collective-permute-start(bf16[512,1,128]{0,2,1:T(8,128)(2,1)S(1)} %collective-permute-done.5), channel_id=1, source_target_pairs={{0,32},{32,64},{64,96},{96,128},{128,160},{160,192},{192,224},{224... | collective-permute-start | bytes 393224 | tf_op jit(solution)/shard_map/ppermute | solution.py:19
  202.4 2.0 collective-permute-start.7
  204.4 5.5 %collective-permute-start.8 = (bf16[512,1,128]{0,2,1:T(8,128)(2,1)S(1)}, bf16[512,1,128]{0,2,1:T(8,128)(2,1)S(1)}, u32[]{:S(2)}, u32[]{:S(2)}) collective-permute-start(bf16[512,1,128]{0,2,1:T(8,128)(2,1)S(1)} %collective-permute-done.7), channel_id=1, source_target_pairs={{0,32},{32,64},{64,96},{96,128},{128,160},{160,192},{192,224},{224... | collective-permute-start | bytes 393224 | tf_op jit(solution)/shard_map/ppermute | solution.py:19
  222.1 5.7 %copy-start = (pred[512,4096]{0,1:T(8,128)(4,1)S(1)}, pred[512,4096]{0,1:T(8,128)(4,1)}, u32[]{:S(2)}) copy-start(pred[512,4096]{0,1:T(8,128)(4,1)} %iota_compare_fusion) | copy-start | bytes 6291460
Sparse Core Ops, SparseCore 0:
  9.8 107.2 all-gather.6
  119.0 35.0 all-gather.8
  156.0 38.8 all-gather.12
  196.5 25.5 all-gather.10
  223.8 34.8 all-gather.16
  261.2 97.6 all-gather.14
